TPU v7x, 256 devices: a whole 4x4x8 slice. The times are simulated.
256 devices in a mesh: occ: 16 (over x_hi, y, core), ao: 16 (over x_lo, z).
Axes of the slice: x: 4 (x_hi: 2, x_lo: 2; x = x_hi * 2 + x_lo), y: 4, z: 8, core: 2. Of those that a mesh axis runs over, the one named last changes fastest.
Arguments:
- coef: bfloat16 [8192, 16], P('ao', 'occ'), may hold values from -0.25 to 0.25
- half_ints: bfloat16 [16, 1024, 8192], P('occ', None, 'ao'), may hold values from -0.5 to 0.5
- metric_inv: bfloat16 [64, 128, 128], replicated, may hold values from -1 to 2, as said below
- dom_blocks: int32 [16, 8], P('occ'), may hold values from 0 to 63, as said below
- dom_len: int32 [16], P('occ'), may hold values from 2 to 8
Outputs:
- exchange_k: float32 [8192, 8192], P('ao', 'occ')
- fit_density: float32 [8192], replicated
Inputs may be any that keep to these rules, and one draw needn't show every extreme that they name: `dom_blocks`: each row holds 8 different block numbers. `metric_inv`: full rank blocks.
All inputs are finite; a program needn't handle non-finite values.
Results may differ from a plain program's by a relative error of at most 0.0055.
Values may be sent and summed in bfloat16 or wider, within the bound.
A program may use at most 128 MiB of HBM per device.

v0:
```python
import jax
import jax.numpy as jnp
from jax import lax
from jax.sharding import PartitionSpec as P


def sent_to_all(x, axis):
    copies = jnp.broadcast_to(x, (lax.axis_size(axis), *x.shape))
    return lax.all_to_all(copies, axis, split_axis=0, concat_axis=0, tiled=True)


def over_copies(x, axis):
    everything = sent_to_all(x, axis)
    return jnp.sum(everything, axis=0)


def on_device(coef, half_ints, metric_inv, dom_blocks, dom_len):
    lmo_count, domain, ao_rows = half_ints.shape
    block = metric_inv.shape[1]
    slots = domain // block
    fit_blocks = metric_inv.shape[0]
    metric_rows = metric_inv[dom_blocks]
    raw_ints = half_ints.reshape(lmo_count, slots, block, ao_rows)
    fitted = jnp.einsum(
        "isab,isbm->isam", metric_rows, raw_ints, preferred_element_type=jnp.float32
    )
    live_slots = jnp.arange(slots, dtype=jnp.int32)[None, :] < dom_len[:, None]
    fitted = jnp.where(live_slots[:, :, None, None], fitted, 0.0)
    fitted = fitted.reshape(lmo_count, domain, ao_rows).astype(jnp.bfloat16)
    pair_part = jnp.einsum("ipm,mi->ip", fitted, coef, preferred_element_type=jnp.float32)
    one_hot = (
        dom_blocks[:, :, None] == jnp.arange(fit_blocks, dtype=jnp.int32)[None, None, :]
    ).astype(jnp.float32)
    pair_sum = over_copies(pair_part, "ao")
    local_density = jnp.einsum("isf,isr->fr", one_hot, pair_sum.reshape(lmo_count, slots, block))
    density = over_copies(local_density, "occ")
    density = density.reshape(fit_blocks * block)
    partial_value = jnp.einsum(
        "ipm,ipn->mn",
        fitted,
        lax.all_gather(fitted, "ao", axis=2, tiled=True),
        preferred_element_type=jnp.float32,
    )
    exchange_k = lax.psum_scatter(partial_value, "occ", scatter_dimension=1, tiled=True)
    return (exchange_k, density)


def solution(mesh):
    in_specs = (P("ao", "occ"), P("occ", None, "ao"), P(), P("occ", None), P("occ"))
    out_specs = (P("ao", "occ"), P())
    return jax.shard_map(
        on_device, mesh=mesh, in_specs=in_specs, out_specs=out_specs, check_vma=False
    )
```

profile of v0, /device:TPU:1, one launch (start us, length us, event | category | flops | bytes accessed | tf_op | source)
XLA Modules:
  0.0 376.6 jit_solution(9049975364195060182)
XLA Ops:
  7.2 0.0 copy-start
  7.2 0.0 all-gather.2.cloned.1.call-start
  8.0 0.7 fusion.7
  8.7 0.1 copy-done
  8.8 0.6 gather_fusion
  9.4 2.6 select_convert_fusion
  12.0 0.0 all-gather.2.cloned.1.call-update
  12.0 0.0 reduce-scatter.2.cloned.1.call-start
  12.1 189.1 %all-gather.2.cloned.1.call-done = bf16[1,1024,8192]{2,1,0:T(8,128)(2,1)} async-done(((bf16[1,1024,512]{2,1,0:T(8,128)(2,1)}), bf16[1,1024,8192]{2,1,0:T(8,128)(2,1)}) %all-gather.2.cloned.1.call-update) | async-done | bytes 16777232 | tf_op jit(solution)/shard_map/all_gather | solution.py:41
  201.2 16.0 %fusion = f32[512,8192]{1,0:T(8,128)} fusion(bf16[1024,512]{1,0:T(8,128)(2,1)} %bitcast.25, bf16[1,1024,8192]{2,1,0:T(8,128)(2,1)} %all-gather.2.cloned.1.call-done), kind=kOutput, calls=%fused_computation.1 | convolution fusion | flops 8589934592 | bytes 34603008 | tf_op jit(solution)/shard_map/ipm,ipn->mn/dot_general | solution.py:38
  217.2 0.0 copy-start.1
  217.2 0.0 copy-start.2
  217.2 0.0 copy-start.3
  217.2 0.0 reduce-scatter.2.cloned.1.call-update
  217.2 1.2 copy-done.1
  218.4 0.0 copy-done.2
  218.4 0.4 fusion.8
  218.8 0.1 broadcast_in_dim.29
  218.8 11.4 %all_to_all.10 = f32[16,1,1024]{2,1,0:T(1,128)S(1)} all-to-all(f32[16,1,1024]{2,1,0:T(1,128)S(1)} %broadcast_in_dim.29), channel_id=1, replica_groups=mesh['occ'=16,'ao'=16] {'ao'}, dimensions={0} | all-to-all | bytes 131072 | tf_op jit(solution)/shard_map/all_to_all | solution.py:9
  230.2 0.1 reduce_sum.18
  230.3 0.0 copy-done.3
  230.3 0.3 fusion.2
  230.6 19.6 %all_to_all.11 = f32[16,64,128]{2,1,0:T(8,128)S(1)} all-to-all(f32[16,64,128]{2,1,0:T(8,128)S(1)} %broadcast_in_dim.30), channel_id=1, replica_groups=mesh['occ'=16,'ao'=16] {'occ'}, dimensions={0} | all-to-all | bytes 1048576 | tf_op jit(solution)/shard_map/all_to_all | solution.py:9
  250.2 0.6 reduce_sum.19
  250.9 118.9 %reduce-scatter.2.cloned.1.call-done = f32[512,512]{1,0:T(8,128)} async-done(((f32[512,8192]{1,0:T(8,128)}), f32[512,512]{1,0:T(8,128)}) %reduce-scatter.2.cloned.1.call-update) | async-done | bytes 1048592 | tf_op jit(solution)/shard_map/reduce_scatter | solution.py:44
  (3 shorter events, 0.1 us)
Async XLA Ops:
  7.2 1.6 copy-start
  7.2 194.0 %all-gather.2.cloned.1.call-start = ((), (), s32[]{:S(2)}) async-start(), calls=%async_computation.3 | async-start | bytes 17825792 | tf_op jit(solution)/shard_map/all_gather | solution.py:41
  12.0 357.7 %reduce-scatter.2.cloned.1.call-start = ((), (), s32[]{:S(2)}) async-start(), calls=%async_computation.4 | async-start | bytes 17825792 | tf_op jit(solution)/shard_map/reduce_scatter | solution.py:44
  217.2 1.2 copy-start.1
  217.2 1.2 copy-start.2
  217.2 13.1 %copy-start.3 = (s32[1,8]{1,0:T(1,128)S(1)}, s32[1,8]{1,0:T(1,128)}, u32[]{:S(2)}) copy-start(s32[1,8]{1,0:T(1,128)} %param.8) | copy-start | bytes 100
Sparse Core Ops, SparseCore 0:
  12.2 189.0 all-gather.1
  217.3 152.3 reduce-scatter.1
where the time goes:
time: 377 us
  waiting for transfers between devices  308 us (82%)
  blocking collectives  31 us (8%)
  matrix products  19.2 us (5%)
  between operations  14.9 us (4%)
    all_gather x1, waiting for transfers between devices, on_device(): lax.all_gather(fitted, 'ao', axis=2, tiled=True)  189 us
    reduce_scatter x1, waiting for transfers between devices, on_device(): lax.psum_scatter(partial_value, 'occ', scatter_dimension=1, tiled=True)  119 us
    all_to_all x2, blocking collectives, sent_to_all(): return lax.all_to_all(copies, axis, split_axis=0, concat_axis=0, tiled=True)  31 us
    dot_general x1, matrix products, on_device(): jnp.einsum('ipm,ipn->mn', fitted, lax.all_gather(fitted, 'ao', axis=2, ti...  16 us
  transfers between devices with their start and end apart: 2, of which 2 were waited for; matrix products, arithmetic and copies ran while one was open for 0% of the time, Pallas kernels for 0%

commit v1 on v0

--- a/solution.py
+++ b/solution.py
@@ -1,7 +1,17 @@
+import functools
 import jax
 import jax.numpy as jnp
 from jax import lax
 from jax.sharding import PartitionSpec as P
+
+
+def update_indices(q_in, axis_key):
+    return jnp.concatenate(
+        lax.all_to_all(jnp.stack([q_in for _ in range(lax.axis_size(axis_key))]), axis_key, 0, 0), 2
+    )
+
+
+remake_weights = functools.partial(update_indices, axis_key="ao")
 
 
 def sent_to_all(x, axis):
@@ -36,10 +46,7 @@
     density = over_copies(local_density, "occ")
     density = density.reshape(fit_blocks * block)
     partial_value = jnp.einsum(
-        "ipm,ipn->mn",
-        fitted,
-        lax.all_gather(fitted, "ao", axis=2, tiled=True),
-        preferred_element_type=jnp.float32,
+        "ipm,ipn->mn", fitted, remake_weights(fitted), preferred_element_type=jnp.float32
     )
     exchange_k = lax.psum_scatter(partial_value, "occ", scatter_dimension=1, tiled=True)
     return (exchange_k, density)

time: 377 us -> 566 us (1.50)
  blocking collectives: 31 us -> 406 us
  waiting for transfers between devices: 308 us -> 119 us
    all_to_all x0 -> x1, blocking collectives: none -> 372 us  [update_indices(): lax.all_to_all(jnp.stack([q_in for _ in range(lax.axis_size(axis_key))]),...]
    all_gather x1 -> x0, waiting for transfers between devices: 189 us -> none  [on_device(): lax.all_gather(fitted, 'ao', axis=2, tiled=True)]
  transfers between devices with their start and end apart: 2 -> 1, of which waited for: 2 -> 1; matrix products, arithmetic and copies ran while one was open for 0% -> 0% of each run, Pallas kernels for 0% -> 0%
where the time goes in v1:
time: 566 us
  blocking collectives  406 us (72%)
  waiting for transfers between devices  119 us (21%)
  matrix products  18 us (3%)
  between operations  14.7 us (3%)
  local copies, waits for them, and re-layouts  6.6 us (1%)
    all_to_all x1, blocking collectives, update_indices(): lax.all_to_all(jnp.stack([q_in for _ in range(lax.axis_size(axis_key))]),...  372 us
    reduce_scatter x1, waiting for transfers between devices, on_device(): lax.psum_scatter(partial_value, 'occ', scatter_dimension=1, tiled=True)  119 us
    all_to_all x2, blocking collectives, sent_to_all(): return lax.all_to_all(copies, axis, split_axis=0, concat_axis=0, tiled=True)  33.5 us
    dot_general x1, matrix products, on_device(): jnp.einsum('ipm,ipn->mn', fitted, remake_weights(fitted), preferred_eleme...  15.7 us
  transfers between devices with their start and end apart: 1, of which 1 were waited for; matrix products, arithmetic and copies ran while one was open for 0% of the time, Pallas kernels for 0%

profile of v1, /device:TPU:1, one launch (start us, length us, event | category | flops | bytes accessed | tf_op | source)
XLA Modules:
  0.0 565.8 jit_solution(4408570215491477101)
XLA Ops:
  7.2 0.0 copy-start
  7.2 0.0 reduce-scatter.2.cloned.1.call-start
  7.2 0.8 fusion.5
  8.7 0.1 copy-done
  8.8 0.6 gather_fusion
  9.4 1.6 select_convert_fusion
  11.0 1.3 copy.12
  12.3 3.9 stack.2
  16.2 372.0 %all_to_all.15 = bf16[16,1,1024,512]{2,3,1,0:T(8,128)(2,1)} all-to-all(bf16[16,1,1024,512]{2,3,1,0:T(8,128)(2,1)S(1)} %stack.2), channel_id=1, replica_groups=mesh['occ'=16,'ao'=16] {'ao'}, dimensions={0} | all-to-all | bytes 33554432 | tf_op jit(solution)/shard_map/all_to_all | solution.py:10
  388.2 15.7 %fusion.6 = f32[512,8192]{1,0:T(8,128)} fusion(bf16[1024,512]{1,0:T(8,128)(2,1)S(1)} %bitcast.28, bf16[1024,8192]{0,1:T(8,128)(2,1)} %bitcast.26), kind=kOutput, calls=%fused_computation.11 | convolution fusion | flops 8589934592 | bytes 34603008 | tf_op jit(solution)/shard_map/ipm,ipn->mn/dot_general | solution.py:48
  403.9 0.0 copy-start.1
  403.9 0.0 copy-start.2
  403.9 0.0 reduce-scatter.2.cloned.1.call-update
  403.9 0.7 copy-done.1
  404.6 0.4 fusion.7
  404.9 0.1 broadcast_in_dim.29
  405.0 13.2 %all_to_all.16 = f32[16,1,1024]{2,1,0:T(1,128)S(1)} all-to-all(f32[16,1,1024]{2,1,0:T(1,128)S(1)} %broadcast_in_dim.29), channel_id=1, replica_groups=mesh['occ'=16,'ao'=16] {'ao'}, dimensions={0} | all-to-all | bytes 131072 | tf_op jit(solution)/shard_map/all_to_all | solution.py:19
  418.2 0.1 reduce_sum.18
  418.2 0.0 copy-done.2
  418.2 0.3 fusion
  418.5 20.4 %all_to_all.17 = f32[16,64,128]{2,1,0:T(8,128)S(1)} all-to-all(f32[16,64,128]{2,1,0:T(8,128)S(1)} %broadcast_in_dim.30), channel_id=1, replica_groups=mesh['occ'=16,'ao'=16] {'occ'}, dimensions={0} | all-to-all | bytes 1048576 | tf_op jit(solution)/shard_map/all_to_all | solution.py:19
  438.9 0.6 reduce_sum.19
  439.6 119.4 %reduce-scatter.2.cloned.1.call-done = f32[512,512]{1,0:T(8,128)} async-done(((f32[512,8192]{1,0:T(8,128)}), f32[512,512]{1,0:T(8,128)}) %reduce-scatter.2.cloned.1.call-update) | async-done | bytes 1048592 | tf_op jit(solution)/shard_map/reduce_scatter | solution.py:51
  (3 shorter events, 0.1 us)
Async XLA Ops:
  7.2 1.6 copy-start
  7.2 551.8 %reduce-scatter.2.cloned.1.call-start = ((), (), s32[]{:S(2)}) async-start(), calls=%async_computation.4 | async-start | bytes 17825792 | tf_op jit(solution)/shard_map/reduce_scatter | solution.py:51
  403.9 0.7 copy-start.1
  403.9 14.3 %copy-start.2 = (s32[1,8]{1,0:T(1,128)S(1)}, s32[1,8]{1,0:T(1,128)}, u32[]{:S(2)}) copy-start(s32[1,8]{1,0:T(1,128)} %param.8) | copy-start | bytes 100
Sparse Core Ops, SparseCore 0:
  404.0 154.9 reduce-scatter.1
